TPU v7x, 32 devices: a whole 2x2x4 slice. The times are simulated.
32 devices in a mesh: row: 4 (over y, x), col: 4 (over z), depth: 2 (over core).
Axes of the slice: x: 2, y: 2, z: 4, core: 2. Of those that a mesh axis runs over, the one named last changes fastest.
Arguments:
- blocks: bfloat16 [128, 12, 128, 128], P(('row', 'col'), None, 'depth'), may hold values from -0.5 to 0.5
- cols: int32 [128, 12], replicated, may hold values from -1 to 127, as said below
- res: int32 [128, 12], replicated, may hold values from 0 to 127, as said below
Outputs:
- purified: bfloat16 [128, 12, 128, 128], P(('row', 'col'), None, None, 'depth')
Inputs may be any that keep to these rules, and one draw needn't show every extreme that they name: `cols`: slots 0 to c-1 of block row i hold distinct columns (i + o) mod 128 with |o| <= 8, slot 0 being i itself; the count c lies between 6 and 12, varies by row, and both ends are reached; the remaining slots hold -1. `res`: block row i keeps 12 distinct columns (i + o) mod 128 with |o| <= 8, the first being i.
All inputs are finite; a program needn't handle non-finite values.
Results may differ from a plain program's by a relative error of at most 0.0044.
Values may be sent and summed in bfloat16 or wider, within the bound.
A program may use at most 64 MiB of HBM per device.

v0:
```python
import functools

import jax
import jax.numpy as jnp
from jax import lax
from jax.experimental import pallas as pl
from jax.experimental.pallas import tpu as pltpu
from jax.sharding import PartitionSpec as P

W = 8
ROWS = 8
LANES = 128
WIDE = 4
MESH = pl.DeviceIdType.MESH
OWN_COLS, OWN_RES, UP_SLOT, DOWN_SLOT, COUNT, META_ROWS = 40, 56, 72, 88, 104, 112


def group_index():
    return lax.axis_index("row") * lax.axis_size("col") + lax.axis_index("col")


def index_kernel(cols_ref, res_ref, meta_ref):
    slots, count = cols_ref.shape
    slots_kept = res_ref.shape[0]
    cols = cols_ref[...]
    res = res_ref[...]
    row = lax.broadcasted_iota(jnp.int32, (slots, count), 1)
    half = count // 2

    def offset(values):
        t = values - row
        t = jnp.where(t > half, t - count, t)
        return jnp.where(t < -half, t + count, t)

    present = cols >= 0
    off = offset(cols)
    in_group = row & (ROWS - 1)
    lane_group = in_group[:1]
    away = 4 * W
    off = jnp.where(present, off, away)
    extra = jnp.full((16 - slots, count), away, jnp.int32)
    off_all = jnp.concatenate([off, extra], axis=0)
    kept_all = jnp.concatenate([offset(res), extra], axis=0)

    def needed(sign):
        need = jnp.zeros((slots, count), jnp.int32)
        for d in range(1, W + 1):
            step = sign * d
            turn = count - d if sign > 0 else d
            kept_there = pltpu.roll(kept_all, turn, 1)
            off_there = pltpu.roll(off_all, turn, 1)
            reads = (kept_there == -step) | (off_there == -step)
            reads = jnp.max(jnp.where(reads, 1, 0), axis=0, keepdims=True)
            if sign > 0:
                inside = lane_group + d >= ROWS
            else:
                inside = lane_group - d < 0
            reads = jnp.where(inside, reads, 0)
            hit = jnp.zeros((slots, count), jnp.int32)
            for q in range(slots_kept):
                hit = jnp.where(off - step == kept_there[q : q + 1], 1, hit)
            need = jnp.maximum(need, hit * reads)
        return present & (need > 0)

    need_up = needed(1)
    need_down = needed(-1)

    def positions(need):
        ones = jnp.where(need, 1, 0)
        run = jnp.zeros((1, count), jnp.int32)
        within = []
        for s in range(slots):
            within.append(run)
            run = run + ones[s : s + 1]
        before = jnp.zeros((1, count), jnp.int32)
        wide = jnp.broadcast_to(run, (8, count))
        for j in range(1, ROWS):
            before = before + jnp.where(lane_group >= j, pltpu.roll(wide, j, 1)[:1], 0)
        return jnp.concatenate([w + before for w in within], axis=0), before + run

    pos_up, total_up = positions(need_up)
    pos_down, total_down = positions(need_down)
    most = jnp.max(jnp.maximum(total_up, total_down))
    which = jnp.int32(0)
    for cap in CAPS[:-1]:
        which = which + jnp.where(most > cap, 1, 0)

    first = group_index() * ROWS
    shift = lax.rem(count - first + ROWS, count)

    def window(values):
        padded = jnp.concatenate(
            [values, jnp.zeros((16 - slots, count), jnp.int32)], axis=0
        )
        return pltpu.roll(padded, shift, 1)[:, :LANES]

    span = ROWS * slots
    empty = 3 * span
    lane = lax.broadcasted_iota(jnp.int32, (16, LANES), 1)
    slot = lax.broadcasted_iota(jnp.int32, (16, LANES), 0)
    up_slot = window(jnp.where(need_up, pos_up, span))
    down_slot = window(jnp.where(need_down, pos_down, span))
    off_w = window(off)
    here = off_w < 4 * W
    place = jnp.where(
        lane < ROWS,
        jnp.where(up_slot < span, span + up_slot, empty),
        jnp.where(
            lane < 2 * ROWS,
            (lane - ROWS) * slots + slot,
            jnp.where(down_slot < span, 2 * span + down_slot, empty),
        ),
    )
    place = jnp.where(here & (lane < 3 * ROWS), place, empty)
    wanted = lax.broadcasted_iota(jnp.int32, (OWN_COLS, LANES), 0) - 2 * W
    dense = jnp.full((OWN_COLS, LANES), empty, jnp.int32)
    for s in range(slots):
        dense = jnp.where(off_w[s : s + 1] == wanted, place[s : s + 1], dense)
    meta_ref[:OWN_COLS] = dense
    reach_col = off_w + lane
    meta_ref[OWN_COLS:OWN_RES] = jnp.where(
        here, (2 * W - reach_col) * LANES + reach_col, LANES - 1
    )
    meta_ref[OWN_RES:UP_SLOT] = window(offset(res)) + lane
    meta_ref[UP_SLOT:DOWN_SLOT] = up_slot
    meta_ref[DOWN_SLOT:COUNT] = down_slot
    meta_ref[COUNT:] = jnp.full((META_ROWS - COUNT, LANES), which, jnp.int32)


def pack_kernel(slots, meta_ref, blocks_ref, up_ref, down_ref):
    @pl.loop(0, slots)
    def _(s):
        for u in range(ROWS):
            block = blocks_ref[u * slots + s]
            up_ref[meta_ref[(UP_SLOT + s) * LANES + ROWS + u]] = block
            down_ref[meta_ref[(DOWN_SLOT + s) * LANES + ROWS + u]] = block


def step_kernel(
    cap,
    chunks,
    slots,
    kept,
    meta_ref,
    blocks_ref,
    up_ref,
    down_ref,
    out_ref,
    table,
    square,
    rounded,
    outgoing,
    own_sem,
    send_sem,
    recv_sem,
    pass_send_sem,
    pass_recv_sem,
    out_send_sem,
    out_recv_sem,
):
    row, col, depth = (lax.axis_index(a) for a in ("row", "col", "depth"))
    row_count, col_count = lax.axis_size("row"), lax.axis_size("col")
    groups = row_count * col_count
    group = row * col_count + col
    following = lax.rem(group + 1, groups)
    preceding = lax.rem(group + groups - 1, groups)
    sibling = (row, col, 1 - depth)
    after = (following // col_count, lax.rem(following, col_count), depth)
    before = (preceding // col_count, lax.rem(preceding, col_count), depth)

    barrier = pltpu.get_barrier_semaphore()
    for device in (sibling, after, before):
        pl.semaphore_signal(barrier, inc=1, device_id=device, device_id_type=MESH)
    pl.semaphore_wait(barrier, 3)

    span = ROWS * slots
    part = cap // chunks
    edge = blocks_ref.shape[1]
    mine = pl.ds(pl.multiple_of(depth * edge, edge), edge)

    halo = []
    for c in range(chunks):
        for way, (source, device) in enumerate(((up_ref, after), (down_ref, before))):
            start = span * (way + 1) + c * part
            k = 2 * c + way
            copy = pltpu.make_async_remote_copy(
                src_ref=source.at[pl.ds(c * part, part)],
                dst_ref=table.at[pl.ds(start, part), mine, :],
                send_sem=send_sem.at[k],
                recv_sem=recv_sem.at[k],
                device_id=device,
                device_id_type=MESH,
            )
            copy.start()
            halo.append((k, start, copy))
    keep = pltpu.make_async_copy(
        blocks_ref, table.at[pl.ds(0, span), mine, :], own_sem.at[0]
    )
    keep.start()
    share = pltpu.make_async_remote_copy(
        src_ref=blocks_ref,
        dst_ref=table.at[pl.ds(0, span), mine, :],
        send_sem=own_sem.at[1],
        recv_sem=own_sem.at[2],
        device_id=sibling,
        device_id_type=MESH,
    )
    share.start()
    table[3 * span] = jnp.zeros(table.shape[1:], table.dtype)
    passed = []
    for k, start, copy in halo:
        copy.wait_recv()
        forward = pltpu.make_async_remote_copy(
            src_ref=table.at[pl.ds(start, part), mine, :],
            dst_ref=table.at[pl.ds(start, part), mine, :],
            send_sem=pass_send_sem.at[k],
            recv_sem=pass_recv_sem.at[k],
            device_id=sibling,
            device_id_type=MESH,
        )
        forward.start()
        passed.append(forward)
    keep.wait()
    share.wait()
    for forward in passed:
        forward.wait()
    for _, _, copy in halo:
        copy.wait_send()

    rows_here = ROWS // 2
    size = table.shape[2]
    even = depth == 0
    half = size // 2

    def right(bases, to):
        return jnp.concatenate(
            [
                jnp.concatenate([table[meta_ref[b + t]] for t in to], axis=1)
                for b in bases
            ],
            axis=0,
        )

    def send_row(r):
        return pltpu.make_async_remote_copy(
            src_ref=outgoing.at[r],
            dst_ref=out_ref.at[depth * rows_here + r],
            send_sem=out_send_sem.at[r],
            recv_sem=out_recv_sem.at[r],
            device_id=sibling,
            device_id_type=MESH,
        )

    @pl.loop(0, rows_here)
    def _(r):
        i = depth * rows_here + r

        def targets(p):
            return [
                meta_ref[(OWN_RES + WIDE * p + e) * LANES + ROWS + i] * LANES
                for e in range(WIDE)
            ]

        @pl.loop(0, kept // WIDE)
        def _(p):
            to = targets(p)
            total = jnp.zeros((size, WIDE * size), jnp.float32)
            for s in range(0, slots, 2):
                left = jnp.concatenate(
                    [table[i * slots + s], table[i * slots + s + 1]], axis=1
                )
                bases = [
                    meta_ref[(OWN_COLS + s + e) * LANES + ROWS + i] for e in range(2)
                ]
                total = total + jnp.dot(
                    left, right(bases, to), preferred_element_type=jnp.float32
                )
            square[p] = total
            rounded[p] = total.astype(jnp.bfloat16)

        @pl.loop(0, kept // WIDE)
        def _(p):
            to = targets(p)
            total = jnp.zeros((size, WIDE * size), jnp.float32)
            for q in range(0, kept, 2):
                bases = [
                    2 * W * LANES
                    - (LANES - 1) * meta_ref[(OWN_RES + q + e) * LANES + ROWS + i]
                    for e in range(2)
                ]
                at = q % WIDE * size
                total = total + jnp.dot(
                    rounded[q // WIDE, :, at : at + 2 * size],
                    right(bases, to),
                    preferred_element_type=jnp.float32,
                )
            value = (3.0 * square[p] - 2.0 * total).astype(jnp.bfloat16)
            for e in range(WIDE):
                turned = value[:, e * size : (e + 1) * size].T
                top, bottom = turned[:half], turned[half:]
                out_ref[i, WIDE * p + e] = jnp.where(even, top, bottom)
                outgoing[r, WIDE * p + e] = jnp.where(even, bottom, top)

        @pl.when(r > 0)
        def _():
            send_row(r - 1).start()

    send_row(rows_here - 1).start()

    @pl.loop(0, rows_here)
    def _(r):
        send_row(r).wait()


def step(cap, chunks, ident, slots, kept, size):
    span = ROWS * slots
    return pl.pallas_call(
        functools.partial(step_kernel, cap, chunks, slots, kept),
        out_shape=jax.ShapeDtypeStruct((ROWS, kept, size // 2, size), jnp.bfloat16),
        in_specs=[pl.BlockSpec(memory_space=pltpu.SMEM)]
        + [pl.BlockSpec(memory_space=pl.ANY)] * 3,
        out_specs=pl.BlockSpec(memory_space=pltpu.VMEM),
        scratch_shapes=[
            pltpu.VMEM((3 * span + 1, size, size), jnp.bfloat16),
            pltpu.VMEM((kept // WIDE, size, WIDE * size), jnp.float32),
            pltpu.VMEM((kept // WIDE, size, WIDE * size), jnp.bfloat16),
            pltpu.VMEM((ROWS // 2, kept, size // 2, size), jnp.bfloat16),
            pltpu.SemaphoreType.DMA((3,)),
            pltpu.SemaphoreType.DMA((2 * chunks,)),
            pltpu.SemaphoreType.DMA((2 * chunks,)),
            pltpu.SemaphoreType.DMA((2 * chunks,)),
            pltpu.SemaphoreType.DMA((2 * chunks,)),
            pltpu.SemaphoreType.DMA((ROWS // 2,)),
            pltpu.SemaphoreType.DMA((ROWS // 2,)),
        ],
        compiler_params=pltpu.CompilerParams(
            collective_id=ident,
            has_side_effects=True,
            vmem_limit_bytes=40 * 2**20,
        ),
        name="step_%d" % cap,
    )


CAPS = (52, 56, 60, 64, 72, 96)


def local(blocks, cols, res):
    rows, slots, edge, size = blocks.shape
    kept = res.shape[1]
    span = rows * slots
    meta = pl.pallas_call(
        index_kernel,
        out_shape=jax.ShapeDtypeStruct((META_ROWS, LANES), jnp.int32),
        name="index",
    )(cols.T, res.T)
    flat = meta.reshape(-1)
    own = blocks.reshape(span, edge, size)
    up, down = pl.pallas_call(
        functools.partial(pack_kernel, slots),
        out_shape=[jax.ShapeDtypeStruct((span + 1, edge, size), blocks.dtype)] * 2,
        in_specs=[
            pl.BlockSpec(memory_space=pltpu.SMEM),
            pl.BlockSpec(memory_space=pltpu.VMEM),
        ],
        name="pack",
    )(flat, own)
    which = meta[COUNT, 0]
    packed = lax.switch(
        which,
        [step(cap, 4, n, slots, kept, size) for n, cap in enumerate(CAPS)],
        flat,
        own,
        up,
        down,
    )
    return jnp.swapaxes(packed, 2, 3)


def solution(mesh):
    return jax.shard_map(
        local,
        mesh=mesh,
        in_specs=(P(("row", "col"), None, "depth", None), P(), P()),
        out_specs=P(("row", "col"), None, None, "depth"),
        check_vma=False,
    )
```

profile of v0, /device:TPU:0, one launch (start us, length us, event | category | flops | bytes accessed | tf_op | source)
XLA Modules:
  0.0 72.2 jit_solution(13691167833430765537)
XLA Ops:
  0.0 0.0 copy-start
  0.0 1.4 %index.1 = s32[112,128]{1,0:T(8,128)S(1)} custom-call(s32[12,128]{1,0:T(8,128)} %bitcast.21, s32[12,128]{1,0:T(8,128)} %bitcast.22), custom_call_target="tpu_custom_call" | custom-call | tf_op jit(solution)/shard_map/index/pallas_call | solution.py:352
  1.4 0.5 slice.4
  2.6 3.2 %pack.1 = (bf16[97,64,128]{2,1,0:T(8,128)(2,1)S(1)}, bf16[97,64,128]{2,1,0:T(8,128)(2,1)}) custom-call(s32[14336]{0:T(1024)S(1)} %bitcast.14, bf16[96,64,128]{2,1,0:T(8,128)(2,1)} %bitcast.6), custom_call_target="tpu_custom_call" | custom-call | tf_op jit(solution)/shard_map/pack/pallas_call | solution.py:359
  5.8 0.0 copy-done
  5.8 63.8 %conditional.1 = (bf16[8,12,64,128]{3,2,1,0:T(8,128)(2,1)}) conditional(s32[]{:T(128)} %bitcast.2, (s32[14336]{0:T(1024)S(1)}, bf16[96,64,128]{2,1,0:T(8,128)(2,1)S(1)}, bf16[97,64,128]{2,1,0:T(8,128)(2,1)S(1)}, bf16[97,64,128]{2,1,0:T(8,128)(2,1)}) %tuple.36, (s32[14336]{0:T(1024)S(1)}, ...), branch_computations={%region_0.0_spmd, %region_1.0_spmd, %region_2.0_spmd, %region_3.0_... | conditional | bytes 8 | solution.py:369
  5.8 63.8 %step_60.1 = bf16[8,12,64,128]{3,2,1,0:T(8,128)(2,1)} custom-call(s32[14336]{0:T(1024)S(1)} %get-tuple-element.68.meta_ref, bf16[96,64,128]{2,1,0:T(8,128)(2,1)S(1)} %get-tuple-element.69.blocks_ref, bf16[97,64,128]{2,1,0:T(8,128)(2,1)S(1)} %get-tuple-element.70.up_ref, bf16[97,64,128]{2,1,0:T(8,128)(2,1)} %get-tuple-element.71.down_ref), custom_call_target="tpu_custom_call" | custom-call | tf_op jit(solution)/shard_map/cond/branch_2_fun/step_60/pallas_call | solution.py:369
  69.6 2.7 %copy.11 = bf16[8,12,128,64]{2,3,1,0:T(8,128)(2,1)} copy(bf16[8,12,128,64]{2,3,1,0:T(8,128)(2,1)} %bitcast.13) | data formatting | bytes 3145728
Async XLA Ops:
  0.0 5.8 %copy-start = (bf16[8,12,64,128]{3,2,1,0:T(8,128)(2,1)S(1)}, bf16[8,12,64,128]{3,2,1,0:T(8,128)(2,1)}, u32[]{:S(2)}) copy-start(bf16[8,12,64,128]{3,2,1,0:T(8,128)(2,1)} %param.9) | copy-start | bytes 4718596
where the time goes:
time: 71.8 us; the launch traced here: 72.2 us
  Pallas kernels  68.4 us (95%)
  local copies, waits for them, and re-layouts  3.19 us (4%)
    pallas_call x1, Pallas kernels, local(): lax.switch(which, [step(cap, 4, n, slots, kept, size) for n, cap in enume...  63.8 us
    pallas_call x1, Pallas kernels, local(): pl.pallas_call(functools.partial(pack_kernel, slots), out_shape=[jax.Shap...  3.2 us
    unnamed x3, local copies, waits for them, and re-layouts  2.67 us

commit v1 on v0

--- a/solution.py
+++ b/solution.py
@@ -138,7 +138,6 @@
 
 def step_kernel(
     cap,
-    chunks,
     slots,
     kept,
     meta_ref,
@@ -174,17 +173,17 @@
     pl.semaphore_wait(barrier, 3)
 
     span = ROWS * slots
-    part = cap // chunks
     edge = blocks_ref.shape[1]
     mine = pl.ds(pl.multiple_of(depth * edge, edge), edge)
 
     halo = []
-    for c in range(chunks):
+    done = 0
+    for c, part in enumerate(pieces(cap)):
         for way, (source, device) in enumerate(((up_ref, after), (down_ref, before))):
-            start = span * (way + 1) + c * part
+            start = span * (way + 1) + done
             k = 2 * c + way
             copy = pltpu.make_async_remote_copy(
-                src_ref=source.at[pl.ds(c * part, part)],
+                src_ref=source.at[pl.ds(done, part)],
                 dst_ref=table.at[pl.ds(start, part), mine, :],
                 send_sem=send_sem.at[k],
                 recv_sem=recv_sem.at[k],
@@ -192,7 +191,8 @@
                 device_id_type=MESH,
             )
             copy.start()
-            halo.append((k, start, copy))
+            halo.append((k, start, part, copy))
+        done += part
     keep = pltpu.make_async_copy(
         blocks_ref, table.at[pl.ds(0, span), mine, :], own_sem.at[0]
     )
@@ -208,7 +208,7 @@
     share.start()
     table[3 * span] = jnp.zeros(table.shape[1:], table.dtype)
     passed = []
-    for k, start, copy in halo:
+    for k, start, part, copy in halo:
         copy.wait_recv()
         forward = pltpu.make_async_remote_copy(
             src_ref=table.at[pl.ds(start, part), mine, :],
@@ -224,7 +224,7 @@
     share.wait()
     for forward in passed:
         forward.wait()
-    for _, _, copy in halo:
+    for _, _, _, copy in halo:
         copy.wait_send()
 
     rows_here = ROWS // 2
@@ -241,12 +241,15 @@
             axis=0,
         )
 
-    def send_row(r):
+    steps = kept // WIDE
+
+    def send(n):
+        at = n % steps * WIDE
         return pltpu.make_async_remote_copy(
-            src_ref=outgoing.at[r],
-            dst_ref=out_ref.at[depth * rows_here + r],
-            send_sem=out_send_sem.at[r],
-            recv_sem=out_recv_sem.at[r],
+            src_ref=outgoing.at[n],
+            dst_ref=out_ref.at[depth * rows_here + n // steps, pl.ds(at, WIDE)],
+            send_sem=out_send_sem.at[n],
+            recv_sem=out_recv_sem.at[n],
             device_id=sibling,
             device_id_type=MESH,
         )
@@ -295,27 +298,30 @@
                     preferred_element_type=jnp.float32,
                 )
             value = (3.0 * square[p] - 2.0 * total).astype(jnp.bfloat16)
+            n = r * steps + p
             for e in range(WIDE):
                 turned = value[:, e * size : (e + 1) * size].T
                 top, bottom = turned[:half], turned[half:]
                 out_ref[i, WIDE * p + e] = jnp.where(even, top, bottom)
-                outgoing[r, WIDE * p + e] = jnp.where(even, bottom, top)
-
-        @pl.when(r > 0)
-        def _():
-            send_row(r - 1).start()
-
-    send_row(rows_here - 1).start()
-
-    @pl.loop(0, rows_here)
-    def _(r):
-        send_row(r).wait()
-
-
-def step(cap, chunks, ident, slots, kept, size):
+                outgoing[n, e] = jnp.where(even, bottom, top)
+
+            @pl.when(n > 0)
+            def _():
+                send(n - 1).start()
+
+    send(rows_here * steps - 1).start()
+
+    @pl.loop(0, rows_here * steps)
+    def _(n):
+        send(n).wait()
+
+
+def step(cap, ident, slots, kept, size):
     span = ROWS * slots
+    chunks = len(pieces(cap))
+    sends = ROWS // 2 * (kept // WIDE)
     return pl.pallas_call(
-        functools.partial(step_kernel, cap, chunks, slots, kept),
+        functools.partial(step_kernel, cap, slots, kept),
         out_shape=jax.ShapeDtypeStruct((ROWS, kept, size // 2, size), jnp.bfloat16),
         in_specs=[pl.BlockSpec(memory_space=pltpu.SMEM)]
         + [pl.BlockSpec(memory_space=pl.ANY)] * 3,
@@ -324,14 +330,14 @@
             pltpu.VMEM((3 * span + 1, size, size), jnp.bfloat16),
             pltpu.VMEM((kept // WIDE, size, WIDE * size), jnp.float32),
             pltpu.VMEM((kept // WIDE, size, WIDE * size), jnp.bfloat16),
-            pltpu.VMEM((ROWS // 2, kept, size // 2, size), jnp.bfloat16),
+            pltpu.VMEM((sends, WIDE, size // 2, size), jnp.bfloat16),
             pltpu.SemaphoreType.DMA((3,)),
             pltpu.SemaphoreType.DMA((2 * chunks,)),
             pltpu.SemaphoreType.DMA((2 * chunks,)),
             pltpu.SemaphoreType.DMA((2 * chunks,)),
             pltpu.SemaphoreType.DMA((2 * chunks,)),
-            pltpu.SemaphoreType.DMA((ROWS // 2,)),
-            pltpu.SemaphoreType.DMA((ROWS // 2,)),
+            pltpu.SemaphoreType.DMA((sends,)),
+            pltpu.SemaphoreType.DMA((sends,)),
         ],
         compiler_params=pltpu.CompilerParams(
             collective_id=ident,
@@ -342,7 +348,12 @@
     )
 
 
-CAPS = (52, 56, 60, 64, 72, 96)
+CAPS = (54, 56, 58, 60, 62, 64, 72, 96)
+
+
+def pieces(cap):
+    head, tail = cap - 16, [8, 4, 4]
+    return [head % 16] * (head % 16 > 0) + [16] * (head // 16) + tail
 
 
 def local(blocks, cols, res):
@@ -368,7 +379,7 @@
     which = meta[COUNT, 0]
     packed = lax.switch(
         which,
-        [step(cap, 4, n, slots, kept, size) for n, cap in enumerate(CAPS)],
+        [step(cap, n, slots, kept, size) for n, cap in enumerate(CAPS)],
         flat,
         own,
         up,

time: 71.8 us -> 72.9 us (1.015)
  no operation moved by 1% of the time
where the time goes in v1:
time: 72.9 us; the launch traced here: 72.7 us
  Pallas kernels  68.9 us (95%)
  local copies, waits for them, and re-layouts  3.19 us (4%)
    pallas_call x1, Pallas kernels, local(): lax.switch(which, [step(cap, n, slots, kept, size) for n, cap in enumerat...  64.2 us
    pallas_call x1, Pallas kernels, local(): pl.pallas_call(functools.partial(pack_kernel, slots), out_shape=[jax.Shap...  3.21 us
    unnamed x3, local copies, waits for them, and re-layouts  2.67 us

profile of v1, /device:TPU:0, one launch (start us, length us, event | category | flops | bytes accessed | tf_op | source)
XLA Modules:
  0.0 72.7 jit_solution(6202195099196798074)
XLA Ops:
  0.0 0.0 copy-start
  0.0 1.4 %index.1 = s32[112,128]{1,0:T(8,128)S(1)} custom-call(s32[12,128]{1,0:T(8,128)} %bitcast.25, s32[12,128]{1,0:T(8,128)} %bitcast.26), custom_call_target="tpu_custom_call" | custom-call | tf_op jit(solution)/shard_map/index/pallas_call | solution.py:363
  1.4 0.5 slice.4
  2.6 3.2 %pack.1 = (bf16[97,64,128]{2,1,0:T(8,128)(2,1)S(1)}, bf16[97,64,128]{2,1,0:T(8,128)(2,1)}) custom-call(s32[14336]{0:T(1024)S(1)} %bitcast.16, bf16[96,64,128]{2,1,0:T(8,128)(2,1)} %bitcast.6), custom_call_target="tpu_custom_call" | custom-call | tf_op jit(solution)/shard_map/pack/pallas_call | solution.py:370
  5.8 0.0 copy-done
  5.8 64.3 %conditional.1 = (bf16[8,12,64,128]{3,2,1,0:T(8,128)(2,1)}) conditional(s32[]{:T(128)} %bitcast.2, (s32[14336]{0:T(1024)S(1)}, bf16[96,64,128]{2,1,0:T(8,128)(2,1)S(1)}, bf16[97,64,128]{2,1,0:T(8,128)(2,1)S(1)}, bf16[97,64,128]{2,1,0:T(8,128)(2,1)}) %tuple.46, (s32[14336]{0:T(1024)S(1)}, ...), branch_computations={%region_0.0_spmd, %region_1.0_spmd, %region_2.0_spmd, %region_3.0_... | conditional | bytes 8 | solution.py:380
  5.8 64.2 %step_58.1 = bf16[8,12,64,128]{3,2,1,0:T(8,128)(2,1)} custom-call(s32[14336]{0:T(1024)S(1)} %get-tuple-element.86.meta_ref, bf16[96,64,128]{2,1,0:T(8,128)(2,1)S(1)} %get-tuple-element.87.blocks_ref, bf16[97,64,128]{2,1,0:T(8,128)(2,1)S(1)} %get-tuple-element.88.up_ref, bf16[97,64,128]{2,1,0:T(8,128)(2,1)} %get-tuple-element.89.down_ref), custom_call_target="tpu_custom_call" | custom-call | tf_op jit(solution)/shard_map/cond/branch_2_fun/step_58/pallas_call | solution.py:380
  70.1 2.7 %copy.13 = bf16[8,12,128,64]{2,3,1,0:T(8,128)(2,1)} copy(bf16[8,12,128,64]{2,3,1,0:T(8,128)(2,1)} %bitcast.15) | data formatting | bytes 3145728
Async XLA Ops:
  0.0 5.8 %copy-start = (bf16[8,12,64,128]{3,2,1,0:T(8,128)(2,1)S(1)}, bf16[8,12,64,128]{3,2,1,0:T(8,128)(2,1)}, u32[]{:S(2)}) copy-start(bf16[8,12,64,128]{3,2,1,0:T(8,128)(2,1)} %param.11) | copy-start | bytes 4718596

commit v2 on v0

--- a/solution.py
+++ b/solution.py
@@ -138,7 +138,6 @@
 
 def step_kernel(
     cap,
-    chunks,
     slots,
     kept,
     meta_ref,
@@ -174,17 +173,17 @@
     pl.semaphore_wait(barrier, 3)
 
     span = ROWS * slots
-    part = cap // chunks
     edge = blocks_ref.shape[1]
     mine = pl.ds(pl.multiple_of(depth * edge, edge), edge)
 
     halo = []
-    for c in range(chunks):
+    done = 0
+    for c, part in enumerate(pieces(cap)):
         for way, (source, device) in enumerate(((up_ref, after), (down_ref, before))):
-            start = span * (way + 1) + c * part
+            start = span * (way + 1) + done
             k = 2 * c + way
             copy = pltpu.make_async_remote_copy(
-                src_ref=source.at[pl.ds(c * part, part)],
+                src_ref=source.at[pl.ds(done, part)],
                 dst_ref=table.at[pl.ds(start, part), mine, :],
                 send_sem=send_sem.at[k],
                 recv_sem=recv_sem.at[k],
@@ -192,7 +191,8 @@
                 device_id_type=MESH,
             )
             copy.start()
-            halo.append((k, start, copy))
+            halo.append((k, start, part, copy))
+        done += part
     keep = pltpu.make_async_copy(
         blocks_ref, table.at[pl.ds(0, span), mine, :], own_sem.at[0]
     )
@@ -208,7 +208,7 @@
     share.start()
     table[3 * span] = jnp.zeros(table.shape[1:], table.dtype)
     passed = []
-    for k, start, copy in halo:
+    for k, start, part, copy in halo:
         copy.wait_recv()
         forward = pltpu.make_async_remote_copy(
             src_ref=table.at[pl.ds(start, part), mine, :],
@@ -224,7 +224,7 @@
     share.wait()
     for forward in passed:
         forward.wait()
-    for _, _, copy in halo:
+    for _, _, _, copy in halo:
         copy.wait_send()
 
     rows_here = ROWS // 2
@@ -312,10 +312,11 @@
         send_row(r).wait()
 
 
-def step(cap, chunks, ident, slots, kept, size):
+def step(cap, ident, slots, kept, size):
     span = ROWS * slots
+    chunks = len(pieces(cap))
     return pl.pallas_call(
-        functools.partial(step_kernel, cap, chunks, slots, kept),
+        functools.partial(step_kernel, cap, slots, kept),
         out_shape=jax.ShapeDtypeStruct((ROWS, kept, size // 2, size), jnp.bfloat16),
         in_specs=[pl.BlockSpec(memory_space=pltpu.SMEM)]
         + [pl.BlockSpec(memory_space=pl.ANY)] * 3,
@@ -342,7 +343,11 @@
     )
 
 
-CAPS = (52, 56, 60, 64, 72, 96)
+CAPS = (54, 56, 58, 60, 62, 64, 72, 96)
+
+
+def pieces(cap):
+    return [cap - 20, 14, 6]
 
 
 def local(blocks, cols, res):
@@ -368,7 +373,7 @@
     which = meta[COUNT, 0]
     packed = lax.switch(
         which,
-        [step(cap, 4, n, slots, kept, size) for n, cap in enumerate(CAPS)],
+        [step(cap, n, slots, kept, size) for n, cap in enumerate(CAPS)],
         flat,
         own,
         up,

time: 71.8 us -> 74.2 us (1.033); the launches traced: 72.2 us -> 73.2 us
  Pallas kernels: 68.4 us -> 69.4 us
    pallas_call x1, Pallas kernels: 63.8 us -> 64.8 us  [local(): lax.switch(which, [step(cap, n, slots, kept, size) for n, cap in enumerat...]
where the time goes in v2:
time: 74.2 us; the launch traced here: 73.2 us
  Pallas kernels  69.4 us (94%)
  local copies, waits for them, and re-layouts  3.19 us (4%)
    pallas_call x1, Pallas kernels, local(): lax.switch(which, [step(cap, n, slots, kept, size) for n, cap in enumerat...  64.8 us
    pallas_call x1, Pallas kernels, local(): pl.pallas_call(functools.partial(pack_kernel, slots), out_shape=[jax.Shap...  3.21 us
    unnamed x3, local copies, waits for them, and re-layouts  2.67 us

profile of v2, /device:TPU:0, one launch (start us, length us, event | category | flops | bytes accessed | tf_op | source)
XLA Modules:
  0.0 73.2 jit_solution(612723056461270648)
XLA Ops:
  0.0 0.0 copy-start
  0.0 1.4 %index.1 = s32[112,128]{1,0:T(8,128)S(1)} custom-call(s32[12,128]{1,0:T(8,128)} %bitcast.25, s32[12,128]{1,0:T(8,128)} %bitcast.26), custom_call_target="tpu_custom_call" | custom-call | tf_op jit(solution)/shard_map/index/pallas_call | solution.py:357
  1.4 0.5 slice.4
  2.6 3.2 %pack.1 = (bf16[97,64,128]{2,1,0:T(8,128)(2,1)S(1)}, bf16[97,64,128]{2,1,0:T(8,128)(2,1)}) custom-call(s32[14336]{0:T(1024)S(1)} %bitcast.16, bf16[96,64,128]{2,1,0:T(8,128)(2,1)} %bitcast.6), custom_call_target="tpu_custom_call" | custom-call | tf_op jit(solution)/shard_map/pack/pallas_call | solution.py:364
  5.8 0.0 copy-done
  5.8 64.8 %conditional.1 = (bf16[8,12,64,128]{3,2,1,0:T(8,128)(2,1)}) conditional(s32[]{:T(128)} %bitcast.2, (s32[14336]{0:T(1024)S(1)}, bf16[96,64,128]{2,1,0:T(8,128)(2,1)S(1)}, bf16[97,64,128]{2,1,0:T(8,128)(2,1)S(1)}, bf16[97,64,128]{2,1,0:T(8,128)(2,1)}) %tuple.46, (s32[14336]{0:T(1024)S(1)}, ...), branch_computations={%region_0.0_spmd, %region_1.0_spmd, %region_2.0_spmd, %region_3.0_... | conditional | bytes 8 | solution.py:374
  5.8 64.8 %step_60.1 = bf16[8,12,64,128]{3,2,1,0:T(8,128)(2,1)} custom-call(s32[14336]{0:T(1024)S(1)} %get-tuple-element.90.meta_ref, bf16[96,64,128]{2,1,0:T(8,128)(2,1)S(1)} %get-tuple-element.91.blocks_ref, bf16[97,64,128]{2,1,0:T(8,128)(2,1)S(1)} %get-tuple-element.92.up_ref, bf16[97,64,128]{2,1,0:T(8,128)(2,1)} %get-tuple-element.93.down_ref), custom_call_target="tpu_custom_call" | custom-call | tf_op jit(solution)/shard_map/cond/branch_3_fun/step_60/pallas_call | solution.py:374
  70.6 2.7 %copy.13 = bf16[8,12,128,64]{2,3,1,0:T(8,128)(2,1)} copy(bf16[8,12,128,64]{2,3,1,0:T(8,128)(2,1)} %bitcast.15) | data formatting | bytes 3145728
Async XLA Ops:
  0.0 5.8 %copy-start = (bf16[8,12,64,128]{3,2,1,0:T(8,128)(2,1)S(1)}, bf16[8,12,64,128]{3,2,1,0:T(8,128)(2,1)}, u32[]{:S(2)}) copy-start(bf16[8,12,64,128]{3,2,1,0:T(8,128)(2,1)} %param.11) | copy-start | bytes 4718596
